TPU v7x, 32 devices: a whole 2x2x4 slice. The times are simulated.
32 devices in a mesh: grp: 2 (over x), pi: 16 (over z, y, core).
Axes of the slice: x: 2, y: 2, z: 4, core: 2. Of those that a mesh axis runs over, the one named last changes fastest.
Arguments:
- left: bfloat16 [128, 1024], P(('grp', 'pi')), parts along dimension 0, may hold values from -6 to 6
- right: bfloat16 [128, 1024], P(('grp', 'pi')), parts along dimension 0, may hold values from -6 to 6
- depth: int32 [128], P(('grp', 'pi')), parts along dimension 0, may hold values from 1 to 32
- w_out: bfloat16 [1024, 128], replicated, may hold values from -0.1875 to 0.1875
- bias: float32 [128], replicated, may hold values from -4 to 4
- pair_cot: bfloat16 [128, 64, 128], P(('grp', 'pi')), parts along dimension 0, may hold values from -6 to 6
Outputs:
- pair_update: bfloat16 [128, 64, 128], P(('grp', 'pi')), parts along dimension 0
- grad_left: float32 [128, 1024], P(('grp', 'pi')), parts along dimension 0
- grad_right: float32 [128, 1024], P(('grp', 'pi')), parts along dimension 0
- grad_w: float32 [2048, 128], P('grp'), parts along dimension 0
- grad_bias: float32 [256], P('grp'), parts along dimension 0
There are 2 independent parts, one for each index of `grp`. A program takes and returns all parts, laid end to end along the dimension named above; an argument that names none is the same for every part. Nothing has to cross between parts.
All inputs are finite; a program needn't handle non-finite values.
Results may differ from a plain program's by a relative error of at most 0.0034.
Values may be sent and summed in bfloat16 or wider, within the bound.
A program may use at most 64 MiB of HBM per device.

v0:
```python
import functools

import jax
import jax.numpy as jnp
from jax import lax
from jax.experimental import pallas as pl
from jax.experimental.pallas import tpu as pltpu
from jax.sharding import PartitionSpec as P

C = 32
EPSILON = 0.001
MESH = pl.DeviceIdType.MESH
F32 = jnp.float32
BF16 = jnp.bfloat16


def split(x):
    high = x.astype(BF16)
    return high, (x - high.astype(F32)).astype(BF16)


def mm(x, y):
    return jnp.dot(x, y, preferred_element_type=F32)


def mm_nt(x, y):
    return lax.dot_general(x, y, (((1,), (1,)), ((), ())), preferred_element_type=F32)


def kernel(
    n, left_ref, right_ref, depth_ref, cot_ref, w_in, bias_ref,
    pu_ref, gl_ref, gr_ref, gw_ref, gb_ref,
    x_ref, w_ref, u_ref, gw_part, gat, bs, uhi, ulo, t_ref, pair_w, got_w, send_w, recv_w,
    part_r, pair_r, got_r, send_r, recv_r, mine_w, all_w,
    send_sems, recv_sems,
):
    me = lax.axis_index("pi")
    rows, width = right_ref.shape
    z = w_in.shape[1]
    samples = width // C
    total = cot_ref.shape[1]
    chunk = gw_ref.shape[1]

    core = lax.rem(me, 2)
    chip = me // 2
    partner = me + 1 - 2 * core
    chips = n // 2

    def copy(k, source, target, peer, slot, sent):
        return pltpu.make_async_remote_copy(
            src_ref=source, dst_ref=target,
            send_sem=send_sems.at[k, sent], recv_sem=recv_sems.at[k, slot],
            device_id={"pi": peer}, device_id_type=MESH,
        )

    def each(act):
        def body(step, carry):
            act(lax.rem(me + 2 * step, n))
            return carry

        lax.fori_loop(1, chips, body, 0)

    def other(p):
        return p + 1 - 2 * core

    def direct(k, source, target, p):
        return copy(k, source, target.at[me], p, me, p)

    def landed(k, target, p):
        return copy(k, target.at[p], target.at[p], partner, p, other(p))

    def gather_start(k, source, target):
        each(lambda p: direct(k, source, target, p).start())
        direct(k, source, target, partner).start()
        target[me] = source[...]

    def gather_pass(k, target):
        def act(p):
            landed(k, target, p).wait_recv()
            landed(k, target, p).start()

        each(act)

    def gather_end(k, target):
        landed(k, target, partner).wait_recv()
        each(lambda p: landed(k, target, other(p)).wait_recv())

    def gather_sent(k, source, target):
        each(lambda p: direct(k, source, target, p).wait_send())
        direct(k, source, target, partner).wait_send()
        each(lambda p: landed(k, target, p).wait_send())

    def pair(index, source, target):
        return copy(4, source.at[1 - core], target, partner, index, index)

    def across(k, source, target, p):
        return copy(k, source.at[p // 2], target.at[chip], p, me, p)

    def across_in(k, source, target, p):
        return copy(k, source.at[p // 2], target.at[p // 2], p, p, p)

    barrier = pltpu.get_barrier_semaphore()

    def greet(p):
        pl.semaphore_signal(barrier, inc=1, device_id={"pi": p}, device_id_type=MESH)

    each(greet)
    greet(partner)
    spot = (rows, rows)
    wide = jnp.broadcast_to(depth_ref[...], spot).astype(F32)
    diagonal = lax.broadcasted_iota(jnp.int32, spot, 0) == lax.broadcasted_iota(jnp.int32, spot, 1)
    own_depth = jnp.sum(jnp.where(diagonal, wide, 0.0), axis=1, keepdims=True)
    x_ref[:, :width] = right_ref[...]
    x_ref[:, width:width + z] = jnp.broadcast_to(own_depth, (rows, z)).astype(BF16)
    cot_sum = jnp.zeros((1, z), F32)
    for i in range(rows):
        cot_sum = cot_sum + jnp.sum(cot_ref[i].astype(F32), axis=0, keepdims=True)
    high, low = split(cot_sum)
    x_ref[:, width + z:] = jnp.concatenate(
        [high.astype(F32), low.astype(F32), jnp.zeros((rows - 2, z), F32)], axis=0
    ).astype(BF16)
    pl.semaphore_wait(barrier, chips)
    gather_start(0, x_ref, gat)

    def sample_of(count):
        return lax.broadcasted_iota(jnp.int32, (count, width), 1) // C

    def kept(count, depths):
        return sample_of(count).astype(F32) < depths

    line = lax.broadcasted_iota(jnp.int32, (samples, width), 0)
    diagonal = sample_of(samples) == line
    own_lines = [
        diagonal & (line.astype(F32) < jnp.broadcast_to(own_depth[i:i + 1], (samples, width)))
        for i in range(rows)
    ]
    fold = (
        lax.broadcasted_iota(jnp.int32, (width, C), 0) % C
        == lax.broadcasted_iota(jnp.int32, (width, C), 1)
    ).astype(F32).astype(BF16)
    unfold = (
        lax.broadcasted_iota(jnp.int32, (C, width), 1) % C
        == lax.broadcasted_iota(jnp.int32, (C, width), 0)
    ).astype(F32).astype(BF16)
    left = left_ref[...].astype(F32)
    spread = [
        jnp.where(own_lines[i], jnp.broadcast_to(left[i:i + 1], (samples, width)), 0.0)
        for i in range(rows)
    ]
    a32 = mm(jnp.concatenate(spread, axis=0).astype(BF16), fold)
    a = a32.astype(BF16)
    w_ref[...] = w_in[...].astype(F32)

    def w_of(d):
        return w_ref[pl.ds(d, C, stride=C), :].astype(BF16)

    for d in range(C):
        product = mm(a, w_of(d))
        for i in range(rows):
            u_ref[pl.ds(i * width + d, samples, stride=C), :] = product[i * samples:(i + 1) * samples]
    for i in range(rows):
        high, low = split(u_ref[i * width:(i + 1) * width])
        uhi[:, i * z:(i + 1) * z] = high
        ulo[:, i * z:(i + 1) * z] = low
    a_t = jnp.concatenate([a32, a32], axis=0).T.astype(BF16)

    gather_pass(0, gat)
    gather_end(0, gat)

    def gather_rows(q, carry):
        both = jnp.concatenate([gat[2 * q].astype(F32), gat[2 * q + 1].astype(F32)], axis=0)
        bs[pl.ds(pl.multiple_of(q * 2 * rows, 2 * rows), 2 * rows), :] = both
        return carry

    lax.fori_loop(0, n // 2, gather_rows, 0)
    depths = bs[:, width:width + z]
    gb_ref[...] = jnp.sum(bs[:, width + z:], axis=0, keepdims=True)
    b32 = jnp.where(
        kept(total, jnp.concatenate([depths] * (width // z), axis=1)), bs[:, :width], 0.0
    )
    b = b32.astype(BF16)
    inverse, highs, lows = [], [], []
    for i in range(rows):
        inverse.append(1.0 / (EPSILON + jnp.minimum(depths, own_depth[i:i + 1])))
        cot = cot_ref[i].astype(F32)
        high, low = split(cot * inverse[i])
        highs.append(high)
        lows.append(low)
    cot_high = jnp.concatenate(highs, axis=1)
    cot_low = jnp.concatenate(lows, axis=1)
    b_t = jnp.concatenate([b32, b32], axis=0).T.astype(BF16)
    t = mm(b_t, jnp.concatenate([cot_high, cot_low], axis=0))
    for i in range(rows):
        t_ref[i * width:(i + 1) * width, :] = t[:, i * z:(i + 1) * z]

    def t_of(d):
        return jnp.concatenate(
            [t_ref[pl.ds(i * width + d, samples, stride=C), :] for i in range(rows)], axis=0
        )

    for d in range(C):
        high, low = split(t_of(d))
        gw_part[pl.ds(d, C, stride=C), :] = mm(a_t, jnp.concatenate([high, low], axis=0))
    for p in range(n):
        pair_w[p % 2, p // 2] = gw_part[p * chunk:(p + 1) * chunk]
    pair(0, pair_w, got_w).start()

    u_high = uhi[...]
    part_r[...] = mm_nt(cot_high, u_high) + mm_nt(cot_low, u_high) + mm_nt(cot_high, ulo[...])

    def scatter_rows(q, carry):
        both = part_r[pl.ds(pl.multiple_of(q * 2 * rows, 2 * rows), 2 * rows), :]
        pair_r[0, q] = both[:rows]
        pair_r[1, q] = both[rows:]
        return carry

    lax.fori_loop(0, chips, scatter_rows, 0)
    pair(1, pair_r, got_r).start()

    pair(0, pair_w, got_w).wait_recv()

    def join_w(m, carry):
        send_w[m] = (pair_w[core, m] + got_w[m]).astype(BF16)
        return carry

    lax.fori_loop(0, chips, join_w, 0)
    each(lambda p: across(1, send_w, recv_w, p).start())
    recv_w[chip] = send_w[chip]

    pair(1, pair_r, got_r).wait_recv()

    def join_r(m, carry):
        send_r[m] = (pair_r[core, m] + got_r[m]).astype(BF16)
        return carry

    lax.fori_loop(0, chips, join_r, 0)
    each(lambda p: across(2, send_r, recv_r, p).start())
    recv_r[chip] = send_r[chip]

    update = mm(b, u_high) + mm(b, ulo[...])
    for i in range(rows):
        pu_ref[i] = (update[:, i * z:(i + 1) * z] * inverse[i] + bias_ref[...]).astype(BF16)

    each(lambda p: across_in(1, send_w, recv_w, p).wait_recv())

    def add_w(m, acc):
        return acc + recv_w[m].astype(F32)

    total_w = lax.fori_loop(0, chips, add_w, jnp.zeros((chunk, z), F32))
    mine_w[...] = total_w.astype(BF16)
    gather_start(3, mine_w, all_w)

    left_acc = jnp.zeros((rows * samples, C), F32)
    for d in range(C):
        high, low = split(t_of(d))
        w_d = w_of(d)
        left_acc = left_acc + mm_nt(
            jnp.concatenate([high, low], axis=1), jnp.concatenate([w_d, w_d], axis=1)
        )
    high, low = split(left_acc)
    lines = mm(high, unfold) + mm(low, unfold)
    for i in range(rows):
        gl_ref[i:i + 1, :] = jnp.sum(
            jnp.where(own_lines[i], lines[i * samples:(i + 1) * samples], 0.0), axis=0, keepdims=True
        )

    gather_pass(3, all_w)
    each(lambda p: across_in(2, send_r, recv_r, p).wait_recv())

    def add_r(m, acc):
        return acc + recv_r[m].astype(F32)

    total_r = lax.fori_loop(0, chips, add_r, jnp.zeros((rows, width), F32))
    gr_ref[...] = jnp.where(kept(rows, jnp.broadcast_to(own_depth, (rows, width))), total_r, 0.0)

    gather_end(3, all_w)
    gw_ref[...] = all_w[...]
    gather_sent(0, x_ref, gat)
    gather_sent(3, mine_w, all_w)
    pair(0, pair_w, got_w).wait_send()
    pair(1, pair_r, got_r).wait_send()
    each(lambda p: across(1, send_w, recv_w, p).wait_send())
    each(lambda p: across(2, send_r, recv_r, p).wait_send())


def finish(*refs):
    half = len(refs) // 2
    for source, target in zip(refs[:half], refs[half:]):
        target[...] = source[...].astype(target.dtype)


def local(n, left, right, depth, w_out, bias, pair_cot):
    rows, width = left.shape
    total, z = pair_cot.shape[1:]
    chunk = w_out.shape[0] // n
    vmem = pl.BlockSpec(memory_space=pltpu.VMEM)
    results = pl.pallas_call(
        functools.partial(kernel, n),
        out_shape=(
            jax.ShapeDtypeStruct((rows, total, z), BF16),
            jax.ShapeDtypeStruct((rows, width), F32),
            jax.ShapeDtypeStruct((rows, width), F32),
            jax.ShapeDtypeStruct((n, chunk, z), BF16),
            jax.ShapeDtypeStruct((1, z), F32),
        ),
        in_specs=[vmem] * 6,
        out_specs=(vmem,) * 5,
        scratch_shapes=[
            pltpu.VMEM((rows, width + 2 * z), BF16),
            pltpu.VMEM((C * C, z), F32),
            pltpu.VMEM((rows * width, z), F32),
            pltpu.VMEM((C * C, z), F32),
            pltpu.VMEM((n, rows, width + 2 * z), BF16),
            pltpu.VMEM((total, width + 2 * z), F32),
            pltpu.VMEM((width, rows * z), BF16),
            pltpu.VMEM((width, rows * z), BF16),
            pltpu.VMEM((rows * width, z), F32),
            pltpu.VMEM((2, n // 2, chunk, z), F32),
            pltpu.VMEM((n // 2, chunk, z), F32),
            pltpu.VMEM((n // 2, chunk, z), BF16),
            pltpu.VMEM((n // 2, chunk, z), BF16),
            pltpu.VMEM((total, width), F32),
            pltpu.VMEM((2, n // 2, rows, width), F32),
            pltpu.VMEM((n // 2, rows, width), F32),
            pltpu.VMEM((n // 2, rows, width), BF16),
            pltpu.VMEM((n // 2, rows, width), BF16),
            pltpu.VMEM((chunk, z), BF16),
            pltpu.VMEM((n, chunk, z), BF16),
            pltpu.SemaphoreType.DMA((5, n)),
            pltpu.SemaphoreType.DMA((5, n)),
        ],
        compiler_params=pltpu.CompilerParams(collective_id=0, has_side_effects=True),
    )(left, right, depth[None, :], pair_cot, w_out, bias[None, :])
    pu, gl, gr, gw, gb = pl.pallas_call(
        finish,
        out_shape=tuple(
            jax.ShapeDtypeStruct(r.shape, F32 if k == 3 else r.dtype) for k, r in enumerate(results)
        ),
        in_specs=[vmem] * 5,
        out_specs=(vmem,) * 5,
    )(*results)
    return pu, gl, gr, gw.reshape(C * C, z), gb.reshape(z)


def solution(mesh):
    placed = (
        P(("grp", "pi"), None),
        P(("grp", "pi"), None),
        P(("grp", "pi")),
        P(),
        P(),
        P(("grp", "pi"), None, None),
    )
    return jax.shard_map(
        functools.partial(local, mesh.shape["pi"]),
        mesh=mesh,
        in_specs=placed,
        out_specs=(
            P(("grp", "pi"), None, None),
            P(("grp", "pi"), None),
            P(("grp", "pi"), None),
            P("grp", None),
            P("grp"),
        ),
        check_vma=False,
    )
```

profile of v0, /device:TPU:0, one launch (start us, length us, event | category | flops | bytes accessed | tf_op | source)
XLA Modules:
  0.0 31.0 jit_solution(58958957284767784)
XLA Ops:
  0.6 28.5 %shard_map.101 = (bf16[4,64,128]{2,1,0:T(8,128)(2,1)}, f32[4,1024]{1,0:T(4,128)}, f32[4,1024]{1,0:T(4,128)}, bf16[16,64,128]{2,1,0:T(8,128)(2,1)}, f32[1,128]{1,0:T(1,128)}) custom-call(bf16[4,1024]{1,0:T(4,128)(2,1)} %left_ref.1, bf16[4,1024]{1,0:T(4,128)(2,1)} %right_ref.1, s32[1,4]{1,0:T(1,128)} %bitcast.4, bf16[4,64,128]{2,1,0:T(8,128)(2,1)} %cot_ref.1, ...), custom_call_target="tpu_custom_call" | custom-call | tf_op jit(solution)/shard_map/pallas_call | solution.py:297
  29.1 1.8 %shard_map.102 = (bf16[4,64,128]{2,1,0:T(8,128)(2,1)}, f32[4,1024]{1,0:T(4,128)}, f32[4,1024]{1,0:T(4,128)}, f32[16,64,128]{2,1,0:T(8,128)}, f32[1,128]{1,0:T(1,128)}) custom-call(bf16[4,64,128]{2,1,0:T(8,128)(2,1)} %get-tuple-element.15.refs_0_, f32[4,1024]{1,0:T(4,128)} %get-tuple-element.16.refs_1_, f32[4,1024]{1,0:T(4,128)} %get-tuple-element.17.refs_2_, ...), custom_call_target="tpu_custom_call" | custom-call | tf_op jit(solution)/shard_map/pallas_call | solution.py:334
where the time goes:
time: 31.4 us; the launch traced here: 31 us
  Pallas kernels  30.3 us (96%)
  between operations  0.64 us (2%)
    pallas_call x1, Pallas kernels, local(): pl.pallas_call(functools.partial(kernel, n), out_shape=(jax.ShapeDtypeStr...  28.5 us
    pallas_call x1, Pallas kernels, local(): pl.pallas_call(finish, out_shape=tuple((jax.ShapeDtypeStruct(r.shape, F32...  1.83 us

commit v1 on v0

v1 whole, which is shorter than its diff:
```python
import functools

import jax
import jax.numpy as jnp
from jax import lax
from jax.experimental import pallas as pl
from jax.experimental.pallas import tpu as pltpu
from jax.sharding import PartitionSpec as P

C = 32
LOW = 8
EPSILON = 0.001
MESH = pl.DeviceIdType.MESH
F32 = jnp.float32
BF16 = jnp.bfloat16
I32 = jnp.int32


def split(x):
    high = x.astype(BF16)
    return high, (x - high.astype(F32)).astype(BF16)


def mm(x, y):
    return jnp.dot(x, y, preferred_element_type=F32)


def mm_nt(x, y):
    return lax.dot_general(x, y, (((1,), (1,)), ((), ())), preferred_element_type=F32)


def iota(shape, axis):
    return lax.broadcasted_iota(I32, shape, axis)


def one_hot(hit):
    return hit.astype(F32).astype(BF16)


def kernel(
    n, left_in, right_in, depth_in, cot_in, w_in, bias_in,
    pu_ref, gl_ref, gr_ref, gw_ref, gb_ref,
    left_v, right_v, depth_v, cot_v, w_v, bias_v,
    xs, gat, xl, lf, b_t, w_ref, o_ref, g_raw, g_ref, send_w, own_w, recv_w, mine_w, all_w,
    send_r, recv_r, r_t, pu_part, pu_got, gl_part, gl_got,
    local_sems, send_sems, recv_sems, ag_sems,
):
    me = lax.axis_index("pi")
    rows, width = right_v.shape
    z = w_v.shape[1]
    samples = width // C
    total = cot_v.shape[2]
    chips = n // 2
    core = lax.rem(me, 2)
    chip = me // 2
    partner = me + 1 - 2 * core
    half = C // 2
    block = LOW * C
    highs = samples // LOW
    part = half * LOW
    q = highs * part
    pairs = rows
    lanes = 2 * total
    chunk = own_w.shape[1]

    bits = [1 << k for k in range((n - 1).bit_length())]
    mine = [lax.rem(me // v, 2) for v in bits]

    def peer(x):
        where = 0
        for v, own in zip(bits, mine):
            where = where + v * lax.rem(own + (x // v) % 2, 2)
        return where

    def each(act, start, stop, step):
        if n <= 32:
            for x in range(start, stop, step):
                act(peer(x))
        else:
            def body(t, carry):
                act(peer(start + step * t))
                return carry

            lax.fori_loop(0, len(range(start, stop, step)), body, 0)

    def everyone(act):
        each(act, n - 1, 0, -1)

    def alike(act):
        each(act, n - 2, 0, -2)

    def copy(k, source, target, p, recv=None):
        return pltpu.make_async_remote_copy(
            src_ref=source, dst_ref=target,
            send_sem=send_sems.at[k], recv_sem=recv_sems.at[k] if recv is None else recv,
            device_id={"pi": p}, device_id_type=MESH,
        )

    def fetch(k, source, target):
        return pltpu.make_async_copy(source, target, local_sems.at[k])

    fetches = [
        fetch(0, right_in, right_v), fetch(1, depth_in, depth_v), fetch(2, cot_in, cot_v.at[core]),
        fetch(3, left_in, left_v), fetch(4, w_in, w_v), fetch(5, bias_in, bias_v),
    ]
    for f in fetches:
        f.start()
    barrier = pltpu.get_barrier_semaphore()
    everyone(
        lambda p: pl.semaphore_signal(barrier, inc=1, device_id={"pi": p}, device_id_type=MESH)
    )

    perm = one_hot(
        (iota((block, block), 0) % C == iota((block, block), 1) // LOW)
        & (iota((block, block), 0) // C == iota((block, block), 1) % LOW)
    )
    fetches[0].wait()
    fetches[1].wait()
    spot = (rows, rows)
    wide = jnp.broadcast_to(depth_v[...], spot).astype(F32)
    own_depth = jnp.sum(
        jnp.where(iota(spot, 0) == iota(spot, 1), wide, 0.0), axis=1, keepdims=True
    )
    kept = (iota((rows, width), 1) // C).astype(F32) < jnp.broadcast_to(own_depth, (rows, width))
    right = jnp.where(kept, right_v[...].astype(F32), 0.0)
    stacked = jnp.concatenate([right[:, h * block:(h + 1) * block] for h in range(highs)], axis=0)
    moved = mm(stacked.astype(BF16), perm)
    for k in range(2):
        for h in range(highs):
            xs[k, :, h * part:(h + 1) * part] = (
                moved[h * rows:(h + 1) * rows, k * part:(k + 1) * part].astype(BF16)
            )
    fetches[2].wait()
    cot_sum = jnp.zeros((1, z), F32)
    for i in range(rows):
        cot_sum = cot_sum + jnp.sum(cot_v[core, i].astype(F32), axis=0, keepdims=True)
    high, low = split(cot_sum)
    spread = jnp.where(
        iota((rows, lanes), 1) % total == me * rows + iota((rows, lanes), 0),
        jnp.broadcast_to(own_depth, (rows, lanes)), 0.0,
    )
    places = jnp.sum(spread, axis=0, keepdims=True)
    parts = [high.astype(F32), low.astype(F32)]
    if lanes > z:
        parts = [jnp.concatenate([v, jnp.zeros((1, lanes - z), F32)], axis=1) for v in parts]
    extra = jnp.concatenate(parts + [places, jnp.zeros((rows - 3, lanes), F32)], axis=0).astype(BF16)
    for k in range(2):
        xs[k, :, q:] = extra
    fetches[3].wait()
    xl[core, :, :width] = jnp.where(kept, left_v[...].astype(F32), 0.0).astype(BF16)
    xl[core, :, width:] = jnp.broadcast_to(own_depth, (rows, z)).astype(BF16)
    gat[me] = xs[core]

    pl.semaphore_wait(barrier, n - 1)
    everyone(lambda p: copy(0, xs.at[lax.rem(p, 2)], gat.at[me], p).start())
    left_copy = copy(1, xl.at[core], xl.at[core], partner)
    cot_copy = copy(2, cot_in, cot_v.at[core], partner)
    left_copy.start()
    cot_copy.start()

    fetches[4].wait()
    fetches[5].wait()
    turned = one_hot(
        (iota((part, block), 1) % C == iota((part, block), 0) // LOW + half * core)
        & (iota((part, block), 1) // C == iota((part, block), 0) % LOW)
    )
    settle = one_hot(
        (iota((part, part), 1) // LOW == iota((part, part), 0) % half)
        & (iota((part, part), 1) % LOW == iota((part, part), 0) // half)
    )
    tops = C // LOW
    moved_w = mm(turned, jnp.concatenate([w_v[t * block:(t + 1) * block] for t in range(tops)], axis=1))
    w_half = jnp.concatenate(
        [moved_w[d * LOW:(d + 1) * LOW, t * z:(t + 1) * z] for d in range(half) for t in range(tops)],
        axis=0,
    )
    w_own = w_half.astype(BF16)
    w_t = w_half.T.astype(BF16)

    left_copy.wait_recv()
    for k in range(2):
        lf[k * rows:(k + 1) * rows] = xl[k].astype(F32)
    diagonal = iota((LOW, block), 1) // C == iota((LOW, block), 0)
    lines = [
        jnp.where(
            diagonal, jnp.broadcast_to(lf[i:i + 1, h * block:(h + 1) * block], (LOW, block)), 0.0
        )
        for i in range(2 * rows) for h in range(highs)
    ]
    fold = one_hot(iota((block, pairs * C), 0) % C == iota((block, pairs * C), 1) % C)
    folded = mm(jnp.concatenate(lines, axis=0).astype(BF16), fold)
    place = iota((samples, pairs * C), 1) // C
    pieces = []
    for i2 in range(2):
        piece = jnp.zeros((samples, pairs * C), F32)
        for p in range(pairs):
            at = (2 * p + i2) * samples
            piece = jnp.where(place == p, folded[at:at + samples], piece)
        pieces.append(piece)
    a_full = jnp.concatenate(pieces, axis=0)
    a = a_full.astype(BF16)
    a_t = a_full.T.astype(BF16)
    first = iota((1, lanes), 1) < total
    own_lanes = [
        jnp.where(
            first,
            jnp.broadcast_to(lf[2 * p:2 * p + 1, width:width + 1], (1, lanes)),
            jnp.broadcast_to(lf[2 * p + 1:2 * p + 2, width:width + 1], (1, lanes)),
        )
        for p in range(pairs)
    ]

    cot_copy.wait_recv()
    cot = cot_v[...].reshape(2 * rows * total, z)
    g_raw[...] = mm_nt(w_own, cot)

    copy(0, gat.at[pl.ds(0, n - 1)], gat.at[pl.ds(0, n - 1)], partner).wait_recv()
    ext = jnp.zeros((rows, lanes), F32)
    for p in range(n):
        ext = ext + gat[p, :, q:].astype(F32)
    gb_ref[...] = ext[0:1, :z] + ext[1:2, :z]
    inverse = [1.0 / (EPSILON + jnp.minimum(ext[2:3], own_lanes[p])) for p in range(pairs)]
    b = jnp.concatenate([gat[p, :, :q].astype(F32) for p in range(n)], axis=0)
    b_t[...] = jnp.concatenate([b, b], axis=0).T
    in_first = iota((samples, lanes), 1) < total
    for d in range(half):
        rows_d = jnp.concatenate(
            [b_t[h * part + d * LOW:h * part + (d + 1) * LOW] for h in range(highs)], axis=0
        )
        w_ref[:samples, d * lanes:(d + 1) * lanes] = jnp.where(in_first, rows_d, 0.0).astype(BF16)
        w_ref[samples:, d * lanes:(d + 1) * lanes] = jnp.where(in_first, 0.0, rows_d).astype(BF16)
    for d in range(0, half, 2):
        product = mm(a_t, w_ref[:, d * lanes:(d + 2) * lanes])
        for e in range(2):
            for p in range(pairs):
                o_ref[(d + e) * C:(d + e + 1) * C, p * lanes:(p + 1) * lanes] = (
                    product[p * C:(p + 1) * C, e * lanes:(e + 1) * lanes] * inverse[p]
                ).astype(BF16)
    gw = mm(o_ref[...], cot)
    gw = jnp.concatenate(
        [
            jnp.concatenate([gw[d * C + t * LOW:d * C + (t + 1) * LOW] for d in range(half)], axis=0)
            for t in range(tops)
        ],
        axis=1,
    )
    gw = mm(settle, gw.astype(BF16))
    for t in range(tops):
        send_w[t * part:(t + 1) * part] = gw[:, t * z:(t + 1) * z].astype(BF16)

    def chunk_of(m):
        return pl.ds(pl.multiple_of(m * chunk, chunk), chunk)

    alike(lambda p: copy(3, send_w.at[chunk_of(p // 2)], recv_w.at[chip], p).start())

    for d in range(half):
        for p in range(pairs):
            g_ref[p * C:(p + 1) * C, d * lanes:(d + 1) * lanes] = (
                g_raw[d * C:(d + 1) * C, p * lanes:(p + 1) * lanes] * inverse[p]
            ).astype(BF16)
    for d in range(0, half, 2):
        product = mm(a, g_ref[:, d * lanes:(d + 2) * lanes])
        for e in range(2):
            view = product[:, e * lanes:(e + 1) * lanes]
            chosen = jnp.where(in_first, view[:samples], view[samples:])
            for h in range(highs):
                r_t[h, (d + e) * LOW:(d + e + 1) * LOW] = chosen[h * LOW:(h + 1) * LOW]
    for h in range(highs):
        flat = r_t[h].T
        flat = (flat[:total] + flat[total:]).astype(BF16)
        for p in range(n):
            send_r[p, :, h * part:(h + 1) * part] = flat[p * rows:(p + 1) * rows]
    everyone(lambda p: copy(4, send_r.at[p], recv_r.at[me], p).start())
    recv_r[me] = send_r[me]

    left_sum = mm_nt(g_ref[...], w_ref[...])
    tall = rows * C // 2
    for k in range(2):
        gl_part[k] = left_sum[k * tall:(k + 1) * tall]
    gl_copy = copy(5, gl_part.at[1 - core], gl_got, partner)
    gl_copy.start()

    update = mm(w_t, o_ref[...])
    for p in range(pairs):
        flat = update[:, p * lanes:(p + 1) * lanes].T
        for e in range(2):
            i = 2 * p + e
            pu_part[i // rows, i % rows] = flat[e * total:(e + 1) * total]
    pu_copy = copy(6, pu_part.at[1 - core], pu_got, partner)
    pu_copy.start()

    own_chunk = send_w[chunk_of(chip)].astype(F32)
    all_recv = copy(3, send_w.at[pl.ds(0, (chips - 1) * chunk)], send_w.at[pl.ds(0, (chips - 1) * chunk)], partner)
    recv_w[chip] = jnp.zeros((chunk, z), BF16)
    all_recv.wait_recv()
    total_w = own_chunk
    for m in range(chips):
        total_w = total_w + recv_w[m].astype(F32)
    mine_w[...] = total_w.astype(BF16)

    def direct(p):
        return copy(7, mine_w, all_w.at[core, chip], p, ag_sems.at[chip])

    def landed(p):
        return copy(8, all_w.at[core, p // 2], all_w.at[core, p // 2], partner)

    alike(lambda p: direct(p).start())
    copy(8, mine_w, all_w.at[core, chip], partner).start()
    all_w[core, chip] = mine_w[...]

    gl_copy.wait_recv()
    owned = gl_part[core] + gl_got[...]
    owned = owned.T
    high, low = split(owned)
    unfold = one_hot(
        (iota((pairs * C // 2, pairs // 2 * block), 0) % C == iota((pairs * C // 2, pairs // 2 * block), 1) % C)
        & (iota((pairs * C // 2, pairs // 2 * block), 0) // C == iota((pairs * C // 2, pairs // 2 * block), 1) // block)
    )
    opened = mm(high, unfold) + mm(low, unfold)
    for p in range(pairs // 2):
        for i2 in range(2):
            for h in range(highs):
                at = i2 * samples + h * LOW
                view = opened[at:at + LOW, p * block:(p + 1) * block]
                gl_ref[2 * p + i2:2 * p + i2 + 1, h * block:(h + 1) * block] = jnp.sum(
                    jnp.where(diagonal, view, 0.0), axis=0, keepdims=True
                )
    gl_ref[...] = jnp.where(kept, gl_ref[...], 0.0)

    pu_copy.wait_recv()
    for i in range(rows):
        pu_ref[i] = (pu_part[core, i] + pu_got[i] + bias_v[...]).astype(BF16)

    copy(4, send_r.at[pl.ds(0, n - 1)], recv_r.at[pl.ds(0, n - 1)], partner).wait_recv()
    sums = []
    for k in range(2):
        acc = jnp.zeros((rows, q), F32)
        for m in range(chips):
            acc = acc + recv_r[2 * m + k].astype(F32)
        sums.append(acc)
    joined = jnp.concatenate(
        [
            jnp.concatenate([sums[k][:, h * part:(h + 1) * part] for k in range(2)], axis=1)
            for h in range(highs)
        ],
        axis=0,
    )
    high, low = split(joined)
    natural = mm_nt(high, perm) + mm_nt(low, perm)
    natural = jnp.concatenate([natural[h * rows:(h + 1) * rows] for h in range(highs)], axis=1)
    gr_ref[...] = jnp.where(kept, natural, 0.0)

    def forward(p):
        pltpu.make_async_remote_copy(
            src_ref=mine_w, dst_ref=all_w.at[core, p // 2],
            send_sem=send_sems.at[7], recv_sem=ag_sems.at[p // 2],
            device_id={"pi": partner}, device_id_type=MESH,
        ).wait_recv()
        landed(p).start()

    each(forward, 2, n, 2)
    copy(8, all_w.at[1 - core], all_w.at[1 - core], partner).wait_recv()
    gw_ref[...] = all_w[...]

    copy(0, gat.at[pl.ds(0, n - 1)], gat.at[pl.ds(0, n - 1)], partner).wait_send()
    left_copy.wait_send()
    cot_copy.wait_send()
    all_recv.wait_send()
    copy(4, send_r.at[pl.ds(0, n - 1)], recv_r.at[pl.ds(0, n - 1)], partner).wait_send()
    gl_copy.wait_send()
    pu_copy.wait_send()
    copy(7, send_w.at[pl.ds(0, (chips - 1) * chunk)], send_w.at[pl.ds(0, (chips - 1) * chunk)], partner).wait_send()
    copy(8, all_w.at[core], all_w.at[core], partner).wait_send()


def finish(pu, gl, gr, gw, gb, pu_out, gl_out, gr_out, gw_out, gb_out):
    pu_out[...] = pu[...]
    gl_out[...] = gl[...]
    gr_out[...] = gr[...]
    gb_out[...] = gb[...]
    half = C // 2
    for k in range(2):
        whole = gw[k].reshape(C * half, gw.shape[-1]).astype(F32)
        for c in range(C):
            gw_out[c * C + k * half:c * C + (k + 1) * half] = whole[c * half:(c + 1) * half]


def local(n, left, right, depth, w_out, bias, pair_cot):
    rows, width = left.shape
    total, z = pair_cot.shape[1:]
    chips = n // 2
    samples = width // C
    q = width // 2
    lanes = 2 * total
    size = C * C // 2
    chunk = size // chips
    vmem = pl.BlockSpec(memory_space=pltpu.VMEM)
    hbm = pl.BlockSpec(memory_space=pl.ANY)
    shapes = (
        jax.ShapeDtypeStruct((rows, total, z), BF16),
        jax.ShapeDtypeStruct((rows, width), F32),
        jax.ShapeDtypeStruct((rows, width), F32),
        jax.ShapeDtypeStruct((2, chips, chunk, z), BF16),
        jax.ShapeDtypeStruct((1, z), F32),
    )
    results = pl.pallas_call(
        functools.partial(kernel, n),
        out_shape=shapes,
        in_specs=[hbm] * 6,
        out_specs=(vmem,) * 5,
        scratch_shapes=[
            pltpu.VMEM((rows, width), BF16),
            pltpu.VMEM((rows, width), BF16),
            pltpu.VMEM((1, rows), jnp.int32),
            pltpu.VMEM((2, rows, total, z), BF16),
            pltpu.VMEM((C * C, z), BF16),
            pltpu.VMEM((1, z), F32),
            pltpu.VMEM((2, rows, q + lanes), BF16),
            pltpu.VMEM((n, rows, q + lanes), BF16),
            pltpu.VMEM((2, rows, width + z), BF16),
            pltpu.VMEM((2 * rows, width + z), F32),
            pltpu.VMEM((q, lanes), F32),
            pltpu.VMEM((2 * samples, C // 2 * lanes), BF16),
            pltpu.VMEM((size, rows * lanes), BF16),
            pltpu.VMEM((size, rows * lanes), F32),
            pltpu.VMEM((rows * C, C // 2 * lanes), BF16),
            pltpu.VMEM((size, z), BF16),
            pltpu.VMEM((1, chunk, z), F32),
            pltpu.VMEM((chips, chunk, z), BF16),
            pltpu.VMEM((chunk, z), BF16),
            pltpu.VMEM((2, chips, chunk, z), BF16),
            pltpu.VMEM((n, rows, q), BF16),
            pltpu.VMEM((n, rows, q), BF16),
            pltpu.VMEM((samples // LOW, C // 2 * LOW, lanes), F32),
            pltpu.VMEM((2, rows, total, z), F32),
            pltpu.VMEM((rows, total, z), F32),
            pltpu.VMEM((2, rows * C // 2, 2 * samples), F32),
            pltpu.VMEM((rows * C // 2, 2 * samples), F32),
            pltpu.SemaphoreType.DMA((6,)),
            pltpu.SemaphoreType.DMA((9,)),
            pltpu.SemaphoreType.DMA((9,)),
            pltpu.SemaphoreType.DMA((chips,)),
        ],
        compiler_params=pltpu.CompilerParams(collective_id=0, has_side_effects=True),
    )(left, right, depth[None, :], pair_cot, w_out, bias[None, :])
    pu, gl, gr, gw, gb = pl.pallas_call(
        finish,
        out_shape=shapes[:3] + (jax.ShapeDtypeStruct((C * C, z), F32),) + shapes[4:],
        in_specs=[vmem] * 5,
        out_specs=(vmem,) * 5,
    )(*results)
    return pu, gl, gr, gw, gb.reshape(z)


def solution(mesh):
    placed = (
        P(("grp", "pi"), None),
        P(("grp", "pi"), None),
        P(("grp", "pi")),
        P(),
        P(),
        P(("grp", "pi"), None, None),
    )
    return jax.shard_map(
        functools.partial(local, mesh.shape["pi"]),
        mesh=mesh,
        in_specs=placed,
        out_specs=(
            P(("grp", "pi"), None, None),
            P(("grp", "pi"), None),
            P(("grp", "pi"), None),
            P("grp", None),
            P("grp"),
        ),
        check_vma=False,
    )
```

time: 31.4 us -> 25.5 us (0.81)
  Pallas kernels: 30.3 us -> 24.7 us
    pallas_call x2, Pallas kernels: 30.3 us -> 24.7 us  [the longest x1 22.8 us: local(): pl.pallas_call(functools.partial(kernel, n), out_shape=shapes, in_specs=[...]
where the time goes in v1:
time: 25.5 us; the launch traced here: 25.3 us
  Pallas kernels  24.7 us (97%)
  between operations  0.64 us (3%)
    pallas_call x1, Pallas kernels, local(): pl.pallas_call(functools.partial(kernel, n), out_shape=shapes, in_specs=[...  22.8 us
    pallas_call x1, Pallas kernels, local(): pl.pallas_call(finish, out_shape=shapes[:3] + (jax.ShapeDtypeStruct((C *...  1.83 us

profile of v1, /device:TPU:0, one launch (start us, length us, event | category | flops | bytes accessed | tf_op | source)
XLA Modules:
  0.0 25.3 jit_solution(14231656514831435193)
XLA Ops:
  0.6 22.8 %shard_map.101 = (bf16[4,64,128]{2,1,0:T(8,128)(2,1)}, f32[4,1024]{1,0:T(4,128)}, f32[4,1024]{1,0:T(4,128)}, bf16[2,8,64,128]{3,2,1,0:T(8,128)(2,1)}, f32[1,128]{1,0:T(1,128)}) custom-call(bf16[4,1024]{1,0:T(4,128)(2,1)} %left_in.1, bf16[4,1024]{1,0:T(4,128)(2,1)} %right_in.1, s32[1,4]{1,0:T(1,128)} %bitcast.3, bf16[4,64,128]{2,1,0:T(8,128)(2,1)} %cot_in.1, ...), custom_call_target="tpu_custom_call" | custom-call | tf_op jit(solution)/shard_map/pallas_call | solution.py:406
  23.5 1.8 %shard_map.102 = (bf16[4,64,128]{2,1,0:T(8,128)(2,1)}, f32[4,1024]{1,0:T(4,128)}, f32[4,1024]{1,0:T(4,128)}, f32[1024,128]{1,0:T(8,128)}, f32[1,128]{1,0:T(1,128)}) custom-call(bf16[4,64,128]{2,1,0:T(8,128)(2,1)} %get-tuple-element.15.pu, f32[4,1024]{1,0:T(4,128)} %get-tuple-element.16.gl, f32[4,1024]{1,0:T(4,128)} %get-tuple-element.17.gr, ...), custom_call_target="tpu_custom_call" | custom-call | tf_op jit(solution)/shard_map/pallas_call | solution.py:446

commit v2 on v1

--- a/solution.py
+++ b/solution.py
@@ -394,8 +394,9 @@
     lanes = 2 * total
     size = C * C // 2
     chunk = size // chips
+    limit = (24 if n <= 32 else 58) * 1024 * 1024
     vmem = pl.BlockSpec(memory_space=pltpu.VMEM)
-    hbm = pl.BlockSpec(memory_space=pl.ANY)
+    hbm = pl.BlockSpec(memory_space=pltpu.HBM)
     shapes = (
         jax.ShapeDtypeStruct((rows, total, z), BF16),
         jax.ShapeDtypeStruct((rows, width), F32),
@@ -403,6 +404,10 @@
         jax.ShapeDtypeStruct((2, chips, chunk, z), BF16),
         jax.ShapeDtypeStruct((1, z), F32),
     )
+    inputs = [
+        pltpu.with_memory_space_constraint(v, pltpu.HBM)
+        for v in (left, right, depth[None, :], pair_cot, w_out, bias[None, :])
+    ]
     results = pl.pallas_call(
         functools.partial(kernel, n),
         out_shape=shapes,
@@ -441,13 +446,14 @@
             pltpu.SemaphoreType.DMA((9,)),
             pltpu.SemaphoreType.DMA((chips,)),
         ],
-        compiler_params=pltpu.CompilerParams(collective_id=0, has_side_effects=True),
-    )(left, right, depth[None, :], pair_cot, w_out, bias[None, :])
+        compiler_params=pltpu.CompilerParams(collective_id=0, has_side_effects=True, vmem_limit_bytes=limit),
+    )(*inputs)
     pu, gl, gr, gw, gb = pl.pallas_call(
         finish,
         out_shape=shapes[:3] + (jax.ShapeDtypeStruct((C * C, z), F32),) + shapes[4:],
         in_specs=[vmem] * 5,
         out_specs=(vmem,) * 5,
+        compiler_params=pltpu.CompilerParams(vmem_limit_bytes=limit),
     )(*results)
     return pu, gl, gr, gw, gb.reshape(z)
 

time: 25.5 us -> 23.7 us (0.929)
  Pallas kernels: 24.7 us -> 22.8 us
    pallas_call x1, Pallas kernels: 1.83 us -> 0.86 us  [local(): pl.pallas_call(finish, out_shape=shapes[:3] + (jax.ShapeDtypeStruct((C *...]
    pallas_call x1, Pallas kernels: 22.8 us -> 22 us  [local(): pl.pallas_call(functools.partial(kernel, n), out_shape=shapes, in_specs=[...]
where the time goes in v2:
time: 23.7 us; the launch traced here: 23.5 us
  Pallas kernels  22.8 us (96%)
  between operations  0.64 us (3%)
    pallas_call x1, Pallas kernels, local(): pl.pallas_call(functools.partial(kernel, n), out_shape=shapes, in_specs=[...  22 us
    pallas_call x1, Pallas kernels, local(): pl.pallas_call(finish, out_shape=shapes[:3] + (jax.ShapeDtypeStruct((C *...  0.86 us

profile of v2, /device:TPU:0, one launch (start us, length us, event | category | flops | bytes accessed | tf_op | source)
XLA Modules:
  0.0 23.5 jit_solution(2562910154975852886)
XLA Ops:
  0.6 22.0 %shard_map.101 = (bf16[4,64,128]{2,1,0:T(8,128)(2,1)S(1)}, f32[4,1024]{1,0:T(4,128)S(1)}, f32[4,1024]{1,0:T(4,128)S(1)}, bf16[2,8,64,128]{3,2,1,0:T(8,128)(2,1)S(1)}, f32[1,128]{1,0:T(1,128)S(1)}) custom-call(bf16[4,1024]{1,0:T(4,128)(2,1)} %left_in.1, bf16[4,1024]{1,0:T(4,128)(2,1)} %right_in.1, s32[1,4]{1,0:T(1,128)} %bitcast.3, ...), custom_call_target="tpu_custom_call" | custom-call | tf_op jit(solution)/shard_map/pallas_call | solution.py:411
  22.6 0.9 %shard_map.102 = (bf16[4,64,128]{2,1,0:T(8,128)(2,1)}, f32[4,1024]{1,0:T(4,128)}, f32[4,1024]{1,0:T(4,128)}, f32[1024,128]{1,0:T(8,128)}, f32[1,128]{1,0:T(1,128)}) custom-call(bf16[4,64,128]{2,1,0:T(8,128)(2,1)S(1)} %get-tuple-element.15.pu, f32[4,1024]{1,0:T(4,128)S(1)} %get-tuple-element.16.gl, f32[4,1024]{1,0:T(4,128)S(1)} %get-tuple-element.17.gr, ...), custom_call_target="tpu_custom_call" | custom-call | tf_op jit(solution)/shard_map/pallas_call | solution.py:451

commit v3 on v2

--- a/solution.py
+++ b/solution.py
@@ -39,9 +39,9 @@
 
 def kernel(
     n, left_in, right_in, depth_in, cot_in, w_in, bias_in,
-    pu_ref, gl_ref, gr_ref, gw_ref, gb_ref,
+    pu_ref, gl_ref, gr_ref, all_w, gb_ref, perm_ref,
     left_v, right_v, depth_v, cot_v, w_v, bias_v,
-    xs, gat, xl, lf, b_t, w_ref, o_ref, g_raw, g_ref, send_w, own_w, recv_w, mine_w, all_w,
+    xs, gat, xl, lf, b_t, w_ref, o_ref, g_raw, g_ref, send_w, recv_w, mine_w,
     send_r, recv_r, r_t, pu_part, pu_got, gl_part, gl_got,
     local_sems, send_sems, recv_sems, ag_sems,
 ):
@@ -61,7 +61,8 @@
     q = highs * part
     pairs = rows
     lanes = 2 * total
-    chunk = own_w.shape[1]
+    stages, span = mine_w.shape[:2]
+    step = half // stages
 
     bits = [1 << k for k in range((n - 1).bit_length())]
     mine = [lax.rem(me // v, 2) for v in bits]
@@ -89,10 +90,10 @@
     def alike(act):
         each(act, n - 2, 0, -2)
 
-    def copy(k, source, target, p, recv=None):
+    def copy(k, source, target, p, recv=None, k_send=None):
         return pltpu.make_async_remote_copy(
             src_ref=source, dst_ref=target,
-            send_sem=send_sems.at[k], recv_sem=recv_sems.at[k] if recv is None else recv,
+            send_sem=send_sems.at[k if k_send is None else k_send], recv_sem=recv_sems.at[k] if recv is None else recv,
             device_id={"pi": p}, device_id_type=MESH,
         )
 
@@ -103,12 +104,14 @@
         fetch(0, right_in, right_v), fetch(1, depth_in, depth_v), fetch(2, cot_in, cot_v.at[core]),
         fetch(3, left_in, left_v), fetch(4, w_in, w_v), fetch(5, bias_in, bias_v),
     ]
-    for f in fetches:
+    for f in fetches[:2]:
         f.start()
     barrier = pltpu.get_barrier_semaphore()
     everyone(
         lambda p: pl.semaphore_signal(barrier, inc=1, device_id={"pi": p}, device_id_type=MESH)
     )
+    for f in fetches[2:]:
+        f.start()
 
     perm = one_hot(
         (iota((block, block), 0) % C == iota((block, block), 1) // LOW)
@@ -125,6 +128,7 @@
     right = jnp.where(kept, right_v[...].astype(F32), 0.0)
     stacked = jnp.concatenate([right[:, h * block:(h + 1) * block] for h in range(highs)], axis=0)
     moved = mm(stacked.astype(BF16), perm)
+    perm_ref[...] = perm
     for k in range(2):
         for h in range(highs):
             xs[k, :, h * part:(h + 1) * part] = (
@@ -163,10 +167,6 @@
     turned = one_hot(
         (iota((part, block), 1) % C == iota((part, block), 0) // LOW + half * core)
         & (iota((part, block), 1) // C == iota((part, block), 0) % LOW)
-    )
-    settle = one_hot(
-        (iota((part, part), 1) // LOW == iota((part, part), 0) % half)
-        & (iota((part, part), 1) % LOW == iota((part, part), 0) // half)
     )
     tops = C // LOW
     moved_w = mm(turned, jnp.concatenate([w_v[t * block:(t + 1) * block] for t in range(tops)], axis=1))
@@ -223,35 +223,24 @@
     b = jnp.concatenate([gat[p, :, :q].astype(F32) for p in range(n)], axis=0)
     b_t[...] = jnp.concatenate([b, b], axis=0).T
     in_first = iota((samples, lanes), 1) < total
-    for d in range(half):
-        rows_d = jnp.concatenate(
-            [b_t[h * part + d * LOW:h * part + (d + 1) * LOW] for h in range(highs)], axis=0
-        )
-        w_ref[:samples, d * lanes:(d + 1) * lanes] = jnp.where(in_first, rows_d, 0.0).astype(BF16)
-        w_ref[samples:, d * lanes:(d + 1) * lanes] = jnp.where(in_first, 0.0, rows_d).astype(BF16)
-    for d in range(0, half, 2):
-        product = mm(a_t, w_ref[:, d * lanes:(d + 2) * lanes])
-        for e in range(2):
-            for p in range(pairs):
-                o_ref[(d + e) * C:(d + e + 1) * C, p * lanes:(p + 1) * lanes] = (
-                    product[p * C:(p + 1) * C, e * lanes:(e + 1) * lanes] * inverse[p]
-                ).astype(BF16)
-    gw = mm(o_ref[...], cot)
-    gw = jnp.concatenate(
-        [
-            jnp.concatenate([gw[d * C + t * LOW:d * C + (t + 1) * LOW] for d in range(half)], axis=0)
-            for t in range(tops)
-        ],
-        axis=1,
-    )
-    gw = mm(settle, gw.astype(BF16))
-    for t in range(tops):
-        send_w[t * part:(t + 1) * part] = gw[:, t * z:(t + 1) * z].astype(BF16)
-
-    def chunk_of(m):
-        return pl.ds(pl.multiple_of(m * chunk, chunk), chunk)
-
-    alike(lambda p: copy(3, send_w.at[chunk_of(p // 2)], recv_w.at[chip], p).start())
+    for h in range(stages):
+        for d in range(h * step, (h + 1) * step):
+            rows_d = jnp.concatenate(
+                [b_t[t * part + d * LOW:t * part + (d + 1) * LOW] for t in range(highs)], axis=0
+            )
+            w_ref[:samples, d * lanes:(d + 1) * lanes] = jnp.where(in_first, rows_d, 0.0).astype(BF16)
+            w_ref[samples:, d * lanes:(d + 1) * lanes] = jnp.where(in_first, 0.0, rows_d).astype(BF16)
+        for d in range(h * step, (h + 1) * step, 2):
+            product = mm(a_t, w_ref[:, d * lanes:(d + 2) * lanes])
+            for e in range(2):
+                for p in range(pairs):
+                    o_ref[(d + e) * C:(d + e + 1) * C, p * lanes:(p + 1) * lanes] = (
+                        product[p * C:(p + 1) * C, e * lanes:(e + 1) * lanes] * inverse[p]
+                    ).astype(BF16)
+        gw = mm(o_ref[h * step * C:(h + 1) * step * C], cot).astype(BF16)
+        for m in range(chips):
+            send_w[h, m] = gw[m * span:(m + 1) * span]
+        alike(lambda p: copy(3 + h, send_w.at[h, p // 2], recv_w.at[h, chip], p, k_send=3).start())
 
     for d in range(half):
         for p in range(pairs):
@@ -270,14 +259,13 @@
         flat = (flat[:total] + flat[total:]).astype(BF16)
         for p in range(n):
             send_r[p, :, h * part:(h + 1) * part] = flat[p * rows:(p + 1) * rows]
-    everyone(lambda p: copy(4, send_r.at[p], recv_r.at[me], p).start())
     recv_r[me] = send_r[me]
 
     left_sum = mm_nt(g_ref[...], w_ref[...])
     tall = rows * C // 2
     for k in range(2):
         gl_part[k] = left_sum[k * tall:(k + 1) * tall]
-    gl_copy = copy(5, gl_part.at[1 - core], gl_got, partner)
+    gl_copy = copy(6, gl_part.at[1 - core], gl_got, partner)
     gl_copy.start()
 
     update = mm(w_t, o_ref[...])
@@ -286,27 +274,33 @@
         for e in range(2):
             i = 2 * p + e
             pu_part[i // rows, i % rows] = flat[e * total:(e + 1) * total]
-    pu_copy = copy(6, pu_part.at[1 - core], pu_got, partner)
+    pu_copy = copy(7, pu_part.at[1 - core], pu_got, partner)
     pu_copy.start()
 
-    own_chunk = send_w[chunk_of(chip)].astype(F32)
-    all_recv = copy(3, send_w.at[pl.ds(0, (chips - 1) * chunk)], send_w.at[pl.ds(0, (chips - 1) * chunk)], partner)
-    recv_w[chip] = jnp.zeros((chunk, z), BF16)
-    all_recv.wait_recv()
-    total_w = own_chunk
-    for m in range(chips):
-        total_w = total_w + recv_w[m].astype(F32)
-    mine_w[...] = total_w.astype(BF16)
-
-    def direct(p):
-        return copy(7, mine_w, all_w.at[core, chip], p, ag_sems.at[chip])
-
-    def landed(p):
-        return copy(8, all_w.at[core, p // 2], all_w.at[core, p // 2], partner)
-
-    alike(lambda p: direct(p).start())
-    copy(8, mine_w, all_w.at[core, chip], partner).start()
-    all_w[core, chip] = mine_w[...]
+    def direct(h, p):
+        return copy(8, mine_w.at[h], all_w.at[core, h, chip], p, ag_sems.at[h, chip])
+
+    def arrived(h, p):
+        return copy(8, mine_w.at[h], all_w.at[core, h, p // 2], partner, ag_sems.at[h, p // 2])
+
+    def landed(h, p):
+        return copy(9, all_w.at[core, h, p // 2], all_w.at[core, h, p // 2], partner)
+
+    for h in range(stages):
+        recv_w[h, chip] = send_w[h, chip]
+    for h in range(stages):
+        copy(
+            3 + h, send_w.at[h, pl.ds(0, chips - 1)], recv_w.at[h, pl.ds(0, chips - 1)], partner, k_send=3
+        ).wait_recv()
+        if h == 0:
+            everyone(lambda p: copy(5, send_r.at[p], recv_r.at[me], p).start())
+        total_w = jnp.zeros((span, z), F32)
+        for m in range(chips):
+            total_w = total_w + recv_w[h, m].astype(F32)
+        mine_w[h] = total_w.astype(BF16)
+        alike(lambda p: direct(h, p).start())
+        copy(9, mine_w.at[h], all_w.at[core, h, chip], partner).start()
+        all_w[core, h, chip] = mine_w[h]
 
     gl_copy.wait_recv()
     owned = gl_part[core] + gl_got[...]
@@ -331,7 +325,7 @@
     for i in range(rows):
         pu_ref[i] = (pu_part[core, i] + pu_got[i] + bias_v[...]).astype(BF16)
 
-    copy(4, send_r.at[pl.ds(0, n - 1)], recv_r.at[pl.ds(0, n - 1)], partner).wait_recv()
+    copy(5, send_r.at[pl.ds(0, n - 1)], recv_r.at[pl.ds(0, n - 1)], partner).wait_recv()
     sums = []
     for k in range(2):
         acc = jnp.zeros((rows, q), F32)
@@ -350,39 +344,43 @@
     natural = jnp.concatenate([natural[h * rows:(h + 1) * rows] for h in range(highs)], axis=1)
     gr_ref[...] = jnp.where(kept, natural, 0.0)
 
-    def forward(p):
-        pltpu.make_async_remote_copy(
-            src_ref=mine_w, dst_ref=all_w.at[core, p // 2],
-            send_sem=send_sems.at[7], recv_sem=ag_sems.at[p // 2],
-            device_id={"pi": partner}, device_id_type=MESH,
-        ).wait_recv()
-        landed(p).start()
-
-    each(forward, 2, n, 2)
-    copy(8, all_w.at[1 - core], all_w.at[1 - core], partner).wait_recv()
-    gw_ref[...] = all_w[...]
+    for h in range(stages):
+        def forward(p):
+            arrived(h, p).wait_recv()
+            landed(h, p).start()
+
+        each(forward, 2, n, 2)
+    copy(9, all_w.at[1 - core], all_w.at[1 - core], partner).wait_recv()
 
     copy(0, gat.at[pl.ds(0, n - 1)], gat.at[pl.ds(0, n - 1)], partner).wait_send()
     left_copy.wait_send()
     cot_copy.wait_send()
-    all_recv.wait_send()
-    copy(4, send_r.at[pl.ds(0, n - 1)], recv_r.at[pl.ds(0, n - 1)], partner).wait_send()
+    copy(3, send_w.at[:, pl.ds(0, chips - 1)], send_w.at[:, pl.ds(0, chips - 1)], partner).wait_send()
+    copy(5, send_r.at[pl.ds(0, n - 1)], recv_r.at[pl.ds(0, n - 1)], partner).wait_send()
     gl_copy.wait_send()
     pu_copy.wait_send()
-    copy(7, send_w.at[pl.ds(0, (chips - 1) * chunk)], send_w.at[pl.ds(0, (chips - 1) * chunk)], partner).wait_send()
-    copy(8, all_w.at[core], all_w.at[core], partner).wait_send()
-
-
-def finish(pu, gl, gr, gw, gb, pu_out, gl_out, gr_out, gw_out, gb_out):
+    copy(8, send_w.at[:, pl.ds(0, chips - 1)], send_w.at[:, pl.ds(0, chips - 1)], partner).wait_send()
+    copy(9, all_w.at[core], all_w.at[core], partner).wait_send()
+
+
+def finish(pu, gl, gr, gw, gb, perm, pu_out, gl_out, gr_out, gw_out, gb_out):
     pu_out[...] = pu[...]
     gl_out[...] = gl[...]
     gr_out[...] = gr[...]
     gb_out[...] = gb[...]
-    half = C // 2
-    for k in range(2):
-        whole = gw[k].reshape(C * half, gw.shape[-1]).astype(F32)
-        for c in range(C):
-            gw_out[c * C + k * half:c * C + (k + 1) * half] = whole[c * half:(c + 1) * half]
+    z = gw.shape[-1]
+    block = LOW * C
+    whole = gw[...].reshape(C * C, z).astype(F32)
+    sides = [
+        jnp.concatenate(
+            [whole[d * C + t * LOW:d * C + (t + 1) * LOW] for d in range(C)], axis=0
+        ).astype(BF16)
+        for t in range(C // LOW)
+    ]
+    for t in range(0, C // LOW, 2):
+        moved = mm(perm[...], jnp.concatenate(sides[t:t + 2], axis=1))
+        for e in range(2):
+            gw_out[(t + e) * block:(t + e + 1) * block] = moved[:, e * z:(e + 1) * z]
 
 
 def local(n, left, right, depth, w_out, bias, pair_cot):
@@ -393,7 +391,9 @@
     q = width // 2
     lanes = 2 * total
     size = C * C // 2
-    chunk = size // chips
+    stages = 2 if size // chips % 16 == 0 else 1
+    piece = size // chips // stages
+    block = LOW * C
     limit = (24 if n <= 32 else 58) * 1024 * 1024
     vmem = pl.BlockSpec(memory_space=pltpu.VMEM)
     hbm = pl.BlockSpec(memory_space=pltpu.HBM)
@@ -401,8 +401,9 @@
         jax.ShapeDtypeStruct((rows, total, z), BF16),
         jax.ShapeDtypeStruct((rows, width), F32),
         jax.ShapeDtypeStruct((rows, width), F32),
-        jax.ShapeDtypeStruct((2, chips, chunk, z), BF16),
+        jax.ShapeDtypeStruct((2, stages, chips, piece, z), BF16),
         jax.ShapeDtypeStruct((1, z), F32),
+        jax.ShapeDtypeStruct((block, block), BF16),
     )
     inputs = [
         pltpu.with_memory_space_constraint(v, pltpu.HBM)
@@ -412,7 +413,7 @@
         functools.partial(kernel, n),
         out_shape=shapes,
         in_specs=[hbm] * 6,
-        out_specs=(vmem,) * 5,
+        out_specs=(vmem,) * 6,
         scratch_shapes=[
             pltpu.VMEM((rows, width), BF16),
             pltpu.VMEM((rows, width), BF16),
@@ -429,11 +430,9 @@
             pltpu.VMEM((size, rows * lanes), BF16),
             pltpu.VMEM((size, rows * lanes), F32),
             pltpu.VMEM((rows * C, C // 2 * lanes), BF16),
-            pltpu.VMEM((size, z), BF16),
-            pltpu.VMEM((1, chunk, z), F32),
-            pltpu.VMEM((chips, chunk, z), BF16),
-            pltpu.VMEM((chunk, z), BF16),
-            pltpu.VMEM((2, chips, chunk, z), BF16),
+            pltpu.VMEM((stages, chips, piece, z), BF16),
+            pltpu.VMEM((stages, chips, piece, z), BF16),
+            pltpu.VMEM((stages, piece, z), BF16),
             pltpu.VMEM((n, rows, q), BF16),
             pltpu.VMEM((n, rows, q), BF16),
             pltpu.VMEM((samples // LOW, C // 2 * LOW, lanes), F32),
@@ -442,16 +441,16 @@
             pltpu.VMEM((2, rows * C // 2, 2 * samples), F32),
             pltpu.VMEM((rows * C // 2, 2 * samples), F32),
             pltpu.SemaphoreType.DMA((6,)),
-            pltpu.SemaphoreType.DMA((9,)),
-            pltpu.SemaphoreType.DMA((9,)),
-            pltpu.SemaphoreType.DMA((chips,)),
+            pltpu.SemaphoreType.DMA((10,)),
+            pltpu.SemaphoreType.DMA((10,)),
+            pltpu.SemaphoreType.DMA((stages, chips)),
         ],
         compiler_params=pltpu.CompilerParams(collective_id=0, has_side_effects=True, vmem_limit_bytes=limit),
     )(*inputs)
     pu, gl, gr, gw, gb = pl.pallas_call(
         finish,
-        out_shape=shapes[:3] + (jax.ShapeDtypeStruct((C * C, z), F32),) + shapes[4:],
-        in_specs=[vmem] * 5,
+        out_shape=shapes[:3] + (jax.ShapeDtypeStruct((C * C, z), F32),) + shapes[4:5],
+        in_specs=[vmem] * 6,
         out_specs=(vmem,) * 5,
         compiler_params=pltpu.CompilerParams(vmem_limit_bytes=limit),
     )(*results)

time: 23.7 us -> 23.2 us (0.979)
  Pallas kernels: 22.8 us -> 22.4 us
    pallas_call x1, Pallas kernels: 22 us -> 21.4 us  [local(): pl.pallas_call(functools.partial(kernel, n), out_shape=shapes, in_specs=[...]
where the time goes in v3:
time: 23.2 us; the launch traced here: 23 us
  Pallas kernels  22.4 us (97%)
  between operations  0.64 us (3%)
    pallas_call x1, Pallas kernels, local(): pl.pallas_call(functools.partial(kernel, n), out_shape=shapes, in_specs=[...  21.4 us
    pallas_call x1, Pallas kernels, local(): pl.pallas_call(finish, out_shape=shapes[:3] + (jax.ShapeDtypeStruct((C *...  1.03 us

profile of v3, /device:TPU:0, one launch (start us, length us, event | category | flops | bytes accessed | tf_op | source)
XLA Modules:
  0.0 23.0 jit_solution(8481144302553262470)
XLA Ops:
  0.6 21.4 %shard_map.101 = (bf16[4,64,128]{2,1,0:T(8,128)(2,1)S(1)}, f32[4,1024]{1,0:T(4,128)S(1)}, f32[4,1024]{1,0:T(4,128)S(1)}, bf16[2,2,8,32,128]{4,3,2,1,0:T(8,128)(2...) custom-call(bf16[4,1024]{1,0:T(4,128)(2,1)} %left_in.1, bf16[4,1024]{1,0:T(4,128)(2,1)} %right_in.1, ...), custom_call_target="tpu_custom_call" | custom-call | tf_op jit(solution)/shard_map/pallas_call | solution.py:412
  22.0 1.0 %shard_map.102 = (bf16[4,64,128]{2,1,0:T(8,128)(2,1)}, f32[4,1024]{1,0:T(4,128)}, f32[4,1024]{1,0:T(4,128)}, f32[1024,128]{1,0:T(8,128)}, f32[1,128]{1,0:T(1,128)}) custom-call(bf16[4,64,128]{2,1,0:T(8,128)(2,1)S(1)} %get-tuple-element.16.pu, f32[4,1024]{1,0:T(4,128)S(1)} %get-tuple-element.17.gl, f32[4,1024]{1,0:T(4,128)S(1)} %get-tuple-element.18.gr, ...), custom_call_target="tpu_custom_call" | custom-call | tf_op jit(solution)/shard_map/pallas_call | solution.py:450

commit v4 on v3

--- a/solution.py
+++ b/solution.py
@@ -292,8 +292,6 @@
         copy(
             3 + h, send_w.at[h, pl.ds(0, chips - 1)], recv_w.at[h, pl.ds(0, chips - 1)], partner, k_send=3
         ).wait_recv()
-        if h == 0:
-            everyone(lambda p: copy(5, send_r.at[p], recv_r.at[me], p).start())
         total_w = jnp.zeros((span, z), F32)
         for m in range(chips):
             total_w = total_w + recv_w[h, m].astype(F32)
@@ -302,6 +300,7 @@
         copy(9, mine_w.at[h], all_w.at[core, h, chip], partner).start()
         all_w[core, h, chip] = mine_w[h]
 
+    everyone(lambda p: copy(5, send_r.at[p], recv_r.at[me], p).start())
     gl_copy.wait_recv()
     owned = gl_part[core] + gl_got[...]
     owned = owned.T
@@ -325,6 +324,12 @@
     for i in range(rows):
         pu_ref[i] = (pu_part[core, i] + pu_got[i] + bias_v[...]).astype(BF16)
 
+    for h in range(stages):
+        def forward(p):
+            arrived(h, p).wait_recv()
+            landed(h, p).start()
+
+        each(forward, 2, n, 2)
     copy(5, send_r.at[pl.ds(0, n - 1)], recv_r.at[pl.ds(0, n - 1)], partner).wait_recv()
     sums = []
     for k in range(2):
@@ -344,12 +349,6 @@
     natural = jnp.concatenate([natural[h * rows:(h + 1) * rows] for h in range(highs)], axis=1)
     gr_ref[...] = jnp.where(kept, natural, 0.0)
 
-    for h in range(stages):
-        def forward(p):
-            arrived(h, p).wait_recv()
-            landed(h, p).start()
-
-        each(forward, 2, n, 2)
     copy(9, all_w.at[1 - core], all_w.at[1 - core], partner).wait_recv()
 
     copy(0, gat.at[pl.ds(0, n - 1)], gat.at[pl.ds(0, n - 1)], partner).wait_send()

time: 23.2 us -> 22.7 us (0.978)
  Pallas kernels: 22.4 us -> 21.9 us
    pallas_call x1, Pallas kernels: 21.4 us -> 20.8 us  [local(): pl.pallas_call(functools.partial(kernel, n), out_shape=shapes, in_specs=[...]
where the time goes in v4:
time: 22.7 us; the launch traced here: 22.5 us
  Pallas kernels  21.9 us (96%)
  between operations  0.64 us (3%)
    pallas_call x1, Pallas kernels, local(): pl.pallas_call(functools.partial(kernel, n), out_shape=shapes, in_specs=[...  20.8 us
    pallas_call x1, Pallas kernels, local(): pl.pallas_call(finish, out_shape=shapes[:3] + (jax.ShapeDtypeStruct((C *...  1.03 us

profile of v4, /device:TPU:0, one launch (start us, length us, event | category | flops | bytes accessed | tf_op | source)
XLA Modules:
  0.0 22.5 jit_solution(6589993430908571370)
XLA Ops:
  0.6 20.8 %shard_map.101 = (bf16[4,64,128]{2,1,0:T(8,128)(2,1)S(1)}, f32[4,1024]{1,0:T(4,128)S(1)}, f32[4,1024]{1,0:T(4,128)S(1)}, bf16[2,2,8,32,128]{4,3,2,1,0:T(8,128)(2...) custom-call(bf16[4,1024]{1,0:T(4,128)(2,1)} %left_in.1, bf16[4,1024]{1,0:T(4,128)(2,1)} %right_in.1, ...), custom_call_target="tpu_custom_call" | custom-call | tf_op jit(solution)/shard_map/pallas_call | solution.py:411
  21.5 1.0 %shard_map.102 = (bf16[4,64,128]{2,1,0:T(8,128)(2,1)}, f32[4,1024]{1,0:T(4,128)}, f32[4,1024]{1,0:T(4,128)}, f32[1024,128]{1,0:T(8,128)}, f32[1,128]{1,0:T(1,128)}) custom-call(bf16[4,64,128]{2,1,0:T(8,128)(2,1)S(1)} %get-tuple-element.16.pu, f32[4,1024]{1,0:T(4,128)S(1)} %get-tuple-element.17.gl, f32[4,1024]{1,0:T(4,128)S(1)} %get-tuple-element.18.gr, ...), custom_call_target="tpu_custom_call" | custom-call | tf_op jit(solution)/shard_map/pallas_call | solution.py:449
